TPU v7x, 32 devices: a whole 2x2x4 slice. The times are simulated.
32 devices in a mesh: cells: 8 (over z, y), grp: 4 (over x, core).
Axes of the slice: x: 2, y: 2, z: 4, core: 2. Of those that a mesh axis runs over, the one named last changes fastest.
Arguments:
- coeffs: bfloat16 [512, 6144], P(('cells', 'grp')), may hold values from -6 to 6
- neighbours: int32 [512, 32], P(('cells', 'grp')), may hold values from 0 to 47
- counts: int32 [512], P(('cells', 'grp')), may hold values from 8 to 32
- boxes: int32 [512], P(('cells', 'grp')), may hold values from 0 to 7
- axial: bfloat16 [512, 32, 96], P(('cells', 'grp')), may hold values from -1 to 1
- rotations: bfloat16 [32, 96, 96], replicated, may hold values from -0.625 to 0.625
- out_map: bfloat16 [96, 96], replicated, may hold values from -0.625 to 0.625
- coupling: bfloat16 [64, 64], replicated, may hold values from -1 to 1, as said below
- in_map: bfloat16 [96, 96], replicated, may hold values from -0.21875 to 0.21875
- tmat: float32 [512, 96], P(('cells', 'grp')), may hold values from -0.5 to 0.5
Outputs:
- product: bfloat16 [512, 6144], P(('cells', 'grp'))
Inputs may be any that keep to these rules, and one draw needn't show every extreme that they name: Entries of coupling are zero on the diagonal.
All inputs are finite; a program needn't handle non-finite values.
Results may differ from a plain program's by a relative error of at most 0.0043.
Values may be sent and summed in bfloat16 or wider, within the bound.
A program may use at most 64 MiB of HBM per device.

v0:
```python
import jax
import jax.numpy as jnp
from jax import lax
from jax.sharding import PartitionSpec as P

NBG = 2


slot_width = 8


def padded(block, sides, width):
    for axis, dim in sides:
        count = lax.axis_size(axis)
        forward = [(i, i + 1) for i in range(count - 1)]
        backward = [(target, source) for source, target in forward]
        low = lax.ppermute(
            lax.slice_in_dim(block, block.shape[dim] - width, None, axis=dim), axis, forward
        )
        high = lax.ppermute(lax.slice_in_dim(block, 0, width, axis=dim), axis, backward)
        block = jnp.concatenate([low, block, high], axis=dim)
    return block


def near_field(cand, nbr, cnt, axial, rot):
    sd, slots = nbr.shape
    width = rot.shape[1]
    incid = cand.shape[1] // width
    groups = slots // slot_width
    live = (lax.broadcasted_iota(jnp.int32, (sd, slots), 1) < cnt[:, None]).astype(jnp.float32)
    scale = axial.astype(jnp.float32) * live[:, :, None]
    idx_groups = nbr.reshape(sd, groups, slot_width).transpose(1, 0, 2)
    scale_groups = scale.reshape(sd, groups, slot_width, width).transpose(1, 0, 2, 3)
    rot_groups = rot.reshape(groups, slot_width, width, width)

    def step(total, item):
        idx, factor, rg = item
        picked = cand[idx].reshape(sd, slot_width, width, incid)
        turned = jnp.einsum("kdc,skcp->skdp", rg, picked, preferred_element_type=jnp.float32)
        scaled = (turned * factor[..., None]).astype(jnp.bfloat16)
        back = jnp.einsum("kdc,skdp->scp", rg, scaled, preferred_element_type=jnp.float32)
        return (total + back, None)

    start = jnp.zeros((sd, width, incid), jnp.float32)
    total, _ = lax.scan(step, start, (idx_groups, scale_groups, rot_groups))
    return total


def apply_tmat(field, tmat):
    half = field.shape[1] // 2
    real_t = tmat[:, :half, None]
    imag_t = tmat[:, half:, None]
    real_u = field[:, :half]
    imag_u = field[:, half:]
    return jnp.concatenate(
        [real_t * real_u - imag_t * imag_u, real_t * imag_u + imag_t * real_u], axis=1
    )


def shards(coeffs, neighbours, counts, boxes, axial, rotations, out_map, coupling, in_map, tmat):
    sd = coeffs.shape[0]
    width = rotations.shape[1]
    incid = coeffs.shape[1] // width
    ngrp = lax.axis_size("grp")
    ncell = lax.axis_size("cells")
    nbc = NBG * ngrp
    column = lax.axis_index("cells")
    cand = padded(coeffs, (("cells", 0),), sd)
    near = near_field(cand, neighbours, counts, axial, rotations)
    onehot = (boxes[:, None] == lax.broadcasted_iota(jnp.int32, (sd, nbc), 1)).astype(jnp.bfloat16)
    partial_sums = lax.dot_general(
        onehot, coeffs, (((0,), (0,)), ((), ())), preferred_element_type=jnp.float32
    )
    summed = lax.psum_scatter(partial_sums, "grp", scatter_dimension=0, tiled=True)
    summed = summed.reshape(NBG, width, incid)
    moments = jnp.einsum(
        "dc,bcp->bdp", out_map.astype(jnp.float32), summed, precision=lax.Precision.HIGHEST
    )
    moments = moments.astype(jnp.bfloat16).reshape(NBG, width * incid)
    rows = lax.dynamic_slice_in_dim(coupling, column * nbc, nbc, 0)
    rows = rows.reshape(nbc, ncell, ngrp, NBG)
    picked_cols = lax.dynamic_slice_in_dim(rows, lax.axis_index("grp"), 1, 2).reshape(
        nbc, ncell * NBG
    )
    partial_local = jnp.dot(
        picked_cols,
        lax.all_gather(moments, "cells", axis=0, tiled=True),
        preferred_element_type=jnp.float32,
    )
    local = lax.psum(partial_local, "grp").astype(jnp.bfloat16)
    chosen = jnp.dot(onehot, local, preferred_element_type=jnp.float32).astype(jnp.bfloat16)
    chosen = chosen.reshape(sd, width, incid)
    far = jnp.einsum("dc,scp->sdp", in_map, chosen, preferred_element_type=jnp.float32)
    field = near + far
    turned = apply_tmat(field, tmat).reshape(sd, width * incid)
    return (coeffs.astype(jnp.float32) - turned).astype(jnp.bfloat16)


def solution(mesh):
    in_specs = (
        P(("cells", "grp"), None),
        P(("cells", "grp"), None),
        P(("cells", "grp")),
        P(("cells", "grp")),
        P(("cells", "grp"), None, None),
        P(),
        P(),
        P(),
        P(),
        P(("cells", "grp"), None),
    )
    out_specs = P(("cells", "grp"), None)
    return jax.shard_map(shards, mesh=mesh, in_specs=in_specs, out_specs=out_specs, check_vma=False)
```

profile of v0, /device:TPU:0, one launch (start us, length us, event | category | flops | bytes accessed | tf_op | source)
XLA Modules:
  0.0 147.4 jit_solution(10058398404660053046)
XLA Ops:
  6.5 0.0 copy-start
  6.5 0.0 copy-start.2
  6.5 0.0 all-reduce.4.cloned.1.call-start
  6.5 1.4 collective-permute-start.1
  8.0 5.5 %collective-permute-start = (bf16[16,6144]{1,0:T(8,128)(2,1)}, bf16[16,6144]{1,0:T(8,128)(2,1)S(1)}, u32[]{:S(2)}, u32[]{:S(2)}) collective-permute-start(bf16[16,6144]{1,0:T(8,128)(2,1)} %param.12), channel_id=1, source_target_pairs={{0,4},{4,8},{8,12},{12,16},{16,20},{20,24},{24,28},{1,5},{5,9},{9,... | collective-permute-start | bytes 589832 | tf_op jit(solution)/shard_map/ppermute | solution.py:17
  13.5 1.9 %fusion.14 = f32[8,6144]{1,0:T(8,128)} fusion(bf16[16,6144]{1,0:T(8,128)(2,1)} %param.12, s32[16]{0:T(128)} %param.15), kind=kOutput, calls=%fused_computation.26 | convolution fusion | flops 1572992 | bytes 393280 | tf_op jit(solution)/shard_map/dot_general | solution.py:71
  15.4 0.0 all-reduce.4.cloned.1.call-update
  15.5 0.8 copy.25
  16.3 0.7 fusion.15
  17.0 0.0 copy-start.1
  17.0 0.7 constant_dynamic-slice_fusion.2
  17.7 0.1 copy.37
  17.8 0.8 fusion.18
  18.7 1.0 multiply_bitcast_fusion
  19.7 1.2 dynamic-slice
  21.5 27.8 %all-reduce.4.cloned.1.call-done = f32[8,6144]{1,0:T(8,128)} async-done(((f32[8,6144]{1,0:T(8,128)}), f32[8,6144]{1,0:T(8,128)}) %all-reduce.4.cloned.1.call-update) | async-done | bytes 196624
  49.2 0.9 constant_dynamic-slice_fusion
  50.2 0.1 reshape.88
  50.3 1.0 fusion.10
  51.3 0.1 copy.29
  51.4 0.1 reshape.102
  51.5 30.8 %all-gather = bf16[8,2,6144]{2,1,0:T(2,128)(2,1)S(1)} all-gather(bf16[1,2,6144]{2,1,0:T(2,128)(2,1)S(1)} %reshape.102), channel_id=1, replica_groups=mesh['cells'=8,'grp'=4] {'cells'}, dimensions={0}, use_global_device_ids=true | all-gather | bytes 221184 | tf_op jit(solution)/shard_map/all_gather | solution.py:87
  82.3 0.1 reshape.103
  82.4 0.2 fusion.19
  82.6 12.6 %all-reduce.5 = bf16[8,6144]{1,0:T(8,128)(2,1)S(1)} all-reduce(f32[8,6144]{1,0:T(8,128)S(1)} %fusion.19), channel_id=1, replica_groups=mesh['cells'=8,'grp'=4] {'grp'}, use_global_device_ids=true, to_apply=%region_3.4 | all-reduce | flops 49152 | bytes 294912 | tf_op jit(solution)/shard_map/psum | solution.py:90
  95.2 0.0 copy-done.2
  95.2 0.2 convolution_convert_fusion
  95.4 0.4 reshape.90
  95.8 0.0 copy-done
  95.8 0.3 convolution_bitcast_fusion
  96.1 0.0 collective-permute-done.1
  96.1 0.0 collective-permute-done
  96.1 0.0 copy-done.1
  96.2 41.5 %while.11 = (s32[]{:T(128)}, f32[16,96,64]{1,2,0:T(8,128)}, s32[4,16,8]{1,2,0:T(8,128)S(1)}, bf16[48,6144]{1,0:T(8,128)(2,1)S(1)}, bf16[4,8,96,96]{3,2,1,0:T(8,1...) while((s32[]{:T(128)}, f32[16,96,64]{1,2,0:T(8,128)}, ...), condition=%wide.region_1.2_spmd.clone, body=%wide.region_0.1_spmd.clone.sunk | while | flops 303760768 | bytes 10905198 | solution.py:45
  96.2 0.1 copy.39
  96.3 0.1 reshape.120
  96.4 1.5 %gather_fusion = bf16[128,6144]{1,0:T(8,128)(2,1)S(1)} fusion(bf16[48,6144]{1,0:T(8,128)(2,1)S(1)} %get-tuple-element.143, s32[1024]{0:T(1024)S(1)} %pad_clamp_fusion.2), kind=kCustom, calls=%fused_computation.clone.clone.1 | custom fusion | bytes 3146240 | tf_op jit(solution)/shard_map/while/body/eval_jaxpr/gather | solution.py:38
  97.9 4.2 %reshape.121 = bf16[16,8,96,64]{3,2,1,0:T(8,128)(2,1)} reshape(bf16[128,6144]{1,0:T(8,128)(2,1)S(1)} %gather_fusion) | data formatting | bytes 3145728 | tf_op jit(solution)/shard_map/while/body/eval_jaxpr/reshape | solution.py:38
  102.1 4.3 %fusion.34 = f32[16,96,64]{1,2,0:T(8,128)} fusion(bf16[16,8,96,64]{3,2,1,0:T(8,128)(2,1)} %reshape.121, f32[16,8,96]{2,1,0:T(8,128)S(1)} %dynamic-slice_bitcast_fusion.2, f32[16,96,64]{1,2,0:T(8,128)} %get-tuple-element.133, pred[]{:T(512)S(6)} %compare.3, bf16[4,8,96,96]{3,2,1,0:T(8,128)(2,1)} %get-tuple-element.144, s32[]{:T(128)S(6)} %copy.42), kind=kOutput, calls=%fused_computation.5.clone.1 | convolution fusion | flops 303759360 | bytes 4507136 | tf_op jit(solution)/shard_map/while/body/eval_jaxpr/kdc,skdp->scp/dot_general | solution.py:41
  106.5 0.1 copy.39
  106.5 0.1 reshape.120
  106.6 1.5 %gather_fusion = bf16[128,6144]{1,0:T(8,128)(2,1)S(1)} fusion(bf16[48,6144]{1,0:T(8,128)(2,1)S(1)} %get-tuple-element.143, s32[1024]{0:T(1024)S(1)} %pad_clamp_fusion.2), kind=kCustom, calls=%fused_computation.clone.clone.1 | custom fusion | bytes 3146240 | tf_op jit(solution)/shard_map/while/body/eval_jaxpr/gather | solution.py:38
  108.1 4.2 %reshape.121 = bf16[16,8,96,64]{3,2,1,0:T(8,128)(2,1)} reshape(bf16[128,6144]{1,0:T(8,128)(2,1)S(1)} %gather_fusion) | data formatting | bytes 3145728 | tf_op jit(solution)/shard_map/while/body/eval_jaxpr/reshape | solution.py:38
  112.4 4.5 %fusion.34 = f32[16,96,64]{1,2,0:T(8,128)} fusion(bf16[16,8,96,64]{3,2,1,0:T(8,128)(2,1)} %reshape.121, f32[16,8,96]{2,1,0:T(8,128)S(1)} %dynamic-slice_bitcast_fusion.2, f32[16,96,64]{1,2,0:T(8,128)} %get-tuple-element.133, pred[]{:T(512)S(6)} %compare.3, bf16[4,8,96,96]{3,2,1,0:T(8,128)(2,1)} %get-tuple-element.144, s32[]{:T(128)S(6)} %copy.42), kind=kOutput, calls=%fused_computation.5.clone.1 | convolution fusion | flops 303759360 | bytes 4507136 | tf_op jit(solution)/shard_map/while/body/eval_jaxpr/kdc,skdp->scp/dot_general | solution.py:41
  116.9 0.1 copy.39
  116.9 0.1 reshape.120
  117.0 1.5 %gather_fusion = bf16[128,6144]{1,0:T(8,128)(2,1)S(1)} fusion(bf16[48,6144]{1,0:T(8,128)(2,1)S(1)} %get-tuple-element.143, s32[1024]{0:T(1024)S(1)} %pad_clamp_fusion.2), kind=kCustom, calls=%fused_computation.clone.clone.1 | custom fusion | bytes 3146240 | tf_op jit(solution)/shard_map/while/body/eval_jaxpr/gather | solution.py:38
  118.5 4.2 %reshape.121 = bf16[16,8,96,64]{3,2,1,0:T(8,128)(2,1)} reshape(bf16[128,6144]{1,0:T(8,128)(2,1)S(1)} %gather_fusion) | data formatting | bytes 3145728 | tf_op jit(solution)/shard_map/while/body/eval_jaxpr/reshape | solution.py:38
  122.8 4.5 %fusion.34 = f32[16,96,64]{1,2,0:T(8,128)} fusion(bf16[16,8,96,64]{3,2,1,0:T(8,128)(2,1)} %reshape.121, f32[16,8,96]{2,1,0:T(8,128)S(1)} %dynamic-slice_bitcast_fusion.2, f32[16,96,64]{1,2,0:T(8,128)} %get-tuple-element.133, pred[]{:T(512)S(6)} %compare.3, bf16[4,8,96,96]{3,2,1,0:T(8,128)(2,1)} %get-tuple-element.144, s32[]{:T(128)S(6)} %copy.42), kind=kOutput, calls=%fused_computation.5.clone.1 | convolution fusion | flops 303759360 | bytes 4507136 | tf_op jit(solution)/shard_map/while/body/eval_jaxpr/kdc,skdp->scp/dot_general | solution.py:41
  127.3 0.1 copy.39
  127.3 0.1 reshape.120
  127.4 1.5 %gather_fusion = bf16[128,6144]{1,0:T(8,128)(2,1)S(1)} fusion(bf16[48,6144]{1,0:T(8,128)(2,1)S(1)} %get-tuple-element.143, s32[1024]{0:T(1024)S(1)} %pad_clamp_fusion.2), kind=kCustom, calls=%fused_computation.clone.clone.1 | custom fusion | bytes 3146240 | tf_op jit(solution)/shard_map/while/body/eval_jaxpr/gather | solution.py:38
  128.9 4.2 %reshape.121 = bf16[16,8,96,64]{3,2,1,0:T(8,128)(2,1)} reshape(bf16[128,6144]{1,0:T(8,128)(2,1)S(1)} %gather_fusion) | data formatting | bytes 3145728 | tf_op jit(solution)/shard_map/while/body/eval_jaxpr/reshape | solution.py:38
  133.2 4.5 %fusion.34 = f32[16,96,64]{1,2,0:T(8,128)} fusion(bf16[16,8,96,64]{3,2,1,0:T(8,128)(2,1)} %reshape.121, f32[16,8,96]{2,1,0:T(8,128)S(1)} %dynamic-slice_bitcast_fusion.2, f32[16,96,64]{1,2,0:T(8,128)} %get-tuple-element.133, pred[]{:T(512)S(6)} %compare.3, bf16[4,8,96,96]{3,2,1,0:T(8,128)(2,1)} %get-tuple-element.144, s32[]{:T(128)S(6)} %copy.42), kind=kOutput, calls=%fused_computation.5.clone.1 | convolution fusion | flops 303759360 | bytes 4507136 | tf_op jit(solution)/shard_map/while/body/eval_jaxpr/kdc,skdp->scp/dot_general | solution.py:41
  137.7 1.1 add.34
  138.8 0.2 multiply_subtract_fusion
  139.0 0.2 pad_maximum_fusion.1
  139.2 0.3 copy.31
  139.5 0.3 reshape.91
  139.8 0.7 subtract_convert_fusion
  (15 shorter events, 0.1 us)
Async XLA Ops:
  6.5 89.3 %copy-start = (bf16[96,96]{1,0:T(8,128)(2,1)S(1)}, bf16[96,96]{1,0:T(8,128)(2,1)}, u32[]{:S(2)}) copy-start(bf16[96,96]{1,0:T(8,128)(2,1)} %param.20) | copy-start | bytes 55300
  6.5 88.6 %copy-start.2 = (s32[16]{0:T(128)S(1)}, s32[16]{0:T(128)}, u32[]{:S(2)}) copy-start(s32[16]{0:T(128)} %param.15) | copy-start | bytes 196
  6.5 42.7 %all-reduce.4.cloned.1.call-start = ((), (), s32[]{:S(2)}) async-start(), calls=%async_computation | async-start | bytes 393216
  6.5 89.6 %collective-permute-start.1 = (bf16[16,6144]{1,0:T(8,128)(2,1)}, bf16[16,6144]{1,0:T(8,128)(2,1)S(1)}, u32[]{:S(2)}, u32[]{:S(2)}) collective-permute-start(bf16[16,6144]{1,0:T(8,128)(2,1)} %param.12), channel_id=1, source_target_pairs={{4,0},{8,4},{12,8},{16,12},{20,16},{24,20},{28,24},{5,1},{9,5},{13... | collective-permute-start | bytes 589832 | tf_op jit(solution)/shard_map/ppermute | solution.py:20
  8.0 88.2 %collective-permute-start = (bf16[16,6144]{1,0:T(8,128)(2,1)}, bf16[16,6144]{1,0:T(8,128)(2,1)S(1)}, u32[]{:S(2)}, u32[]{:S(2)}) collective-permute-start(bf16[16,6144]{1,0:T(8,128)(2,1)} %param.12), channel_id=1, source_target_pairs={{0,4},{4,8},{8,12},{12,16},{16,20},{20,24},{24,28},{1,5},{5,9},{9,... | collective-permute-start | bytes 589832 | tf_op jit(solution)/shard_map/ppermute | solution.py:17
  17.0 79.1 %copy-start.1 = (bf16[16,6144]{1,0:T(8,128)(2,1)S(1)}, bf16[16,6144]{1,0:T(8,128)(2,1)}, u32[]{:S(2)}) copy-start(bf16[16,6144]{1,0:T(8,128)(2,1)} %param.12) | copy-start | bytes 589828
Sparse Core Ops, SparseCore 0:
  15.6 33.6 all-reduce.3
where the time goes:
time: 148 us; the launch traced here: 147 us
  blocking collectives  43.3 us (29%)
  local copies, waits for them, and re-layouts  29.5 us (20%)
  waiting for transfers between devices  27.8 us (19%)
  matrix products  21.4 us (14%)
  between operations  14.1 us (10%)
  starting transfers between devices  6.96 us (5%)
  other arithmetic  4.14 us (3%)
    all_gather x1, blocking collectives, shards(): lax.all_gather(moments, 'cells', axis=0, tiled=True)  30.8 us
    unnamed x2, waiting for transfers between devices  27.8 us
    dot_general x4, matrix products, step(): jnp.einsum('kdc,skdp->scp', rg, scaled, preferred_element_type=jnp.float32)  17.8 us
    reshape x4, local copies, waits for them, and re-layouts, step(): picked = cand[idx].reshape(sd, slot_width, width, incid)  16.9 us
    psum x1, blocking collectives, shards(): local = lax.psum(partial_local, 'grp').astype(jnp.bfloat16)  12.6 us
    gather x4, local copies, waits for them, and re-layouts, step(): picked = cand[idx].reshape(sd, slot_width, width, incid)  5.95 us
    ppermute x1, starting transfers between devices, padded(): lax.ppermute(lax.slice_in_dim(block, block.shape[dim] - width, None, axis...  5.54 us
    unnamed x12, local copies, waits for them, and re-layouts  3.24 us
  transfers between devices with their start and end apart: 3, of which 1 were waited for; matrix products, arithmetic and copies ran while one was open for 7% of the time, Pallas kernels for 0%

commit v1 on v0

v1 whole, which is shorter than its diff:
```python
import functools

import jax
import jax.numpy as jnp
from jax import lax
from jax.experimental import pallas as pl
from jax.experimental.pallas import tpu as pltpu
from jax.sharding import PartitionSpec as P

NBG = 2
MESH = pl.DeviceIdType.MESH
F32 = jnp.float32
BF16 = jnp.bfloat16


def dot_nt(a, b):
    return lax.dot_general(a, b, (((1,), (1,)), ((), ())), preferred_element_type=F32)


def kernel(dims, nbr_ref, cnt_ref, box_ref, x_ref, axial_ref, rot_ref, out_map_ref, coup_ref, in_map_ref, tmat_ref,
           o_ref, cand, w_pair, w_stack, scale, acc, sums, part, arrived, mom, mall, lhs_c, loc, ball, farbuf, maps,
           h_send, h_recv, f_send, f_recv, a_send, a_recv, m_send, m_recv, l_send, l_recv):
    ncell, ngrp, chunks, sd, slots, width, incid, lanes, nbc, pq = dims
    half = width // 2
    rows = nbc * pq
    pairs = slots // 2
    n = lax.axis_index("cells")
    g = lax.axis_index("grp")
    par = n % 2
    partner = n + 1 - 2 * par
    onward = n + 2 - 4 * par
    source = n - 2 + 4 * par
    forwards = jnp.logical_and(onward >= 0, onward < ncell)
    receives = jnp.logical_and(source >= 0, source < ncell)
    near_slot = 2 * (1 - par)
    other_slot = 2 * par
    step = sd // chunks

    def cell(d):
        return lax.rem(n + d, ncell)

    def member(d):
        return lax.rem(g + d, ngrp)

    barrier = pltpu.get_barrier_semaphore()
    for d in range(1, ncell):
        pl.semaphore_signal(barrier, inc=1, device_id=(cell(d), g), device_id_type=MESH)
    for d in range(1, ngrp):
        pl.semaphore_signal(barrier, inc=1, device_id=(n, member(d)), device_id_type=MESH)
    pl.semaphore_wait(barrier, ncell + ngrp - 2)

    def swap(h):
        return pltpu.make_async_remote_copy(
            src_ref=x_ref.at[pl.ds(h * step, step)], dst_ref=cand.at[pl.ds(other_slot * sd + h * step, step)],
            send_sem=h_send.at[h], recv_sem=h_recv.at[h], device_id=(partner, g), device_id_type=MESH)

    def forward(h):
        return pltpu.make_async_remote_copy(
            src_ref=cand.at[pl.ds(near_slot * sd + h * step, step)],
            dst_ref=cand.at[pl.ds(other_slot * sd + h * step, step)],
            send_sem=f_send.at[h], recv_sem=f_recv.at[h], device_id=(onward, g), device_id_type=MESH)

    for h in range(chunks):
        swap(h).start()

    xs = [x_ref[s].astype(F32) for s in range(sd)]
    for b in range(nbc):
        total = None
        for s in range(sd):
            term = xs[s] * jnp.where(box_ref[s] == b, 1.0, 0.0)
            total = term if total is None else total + term
        for q in range(ngrp):
            sums[q, b * pq:(b + 1) * pq, :] = total[q * pq:(q + 1) * pq]
    for q in range(ngrp):
        part[q] = sums[q].astype(BF16)

    def spread(d):
        return pltpu.make_async_remote_copy(
            src_ref=part.at[member(d)], dst_ref=arrived.at[d], send_sem=a_send.at[d], recv_sem=a_recv.at[d],
            device_id=(n, member(d)), device_id_type=MESH)

    for d in range(1, ngrp):
        spread(d).start()

    cand[sd:2 * sd] = x_ref[...]

    @pl.when(jnp.logical_not(receives))
    def _():
        cand[pl.ds(other_slot * sd, sd)] = jnp.zeros((sd, incid, lanes), BF16)

    for m, ref in enumerate((out_map_ref, in_map_ref)):
        maps[m] = jnp.zeros((lanes, lanes), BF16)
        maps[m, :width, :width] = ref[...]

    for d in range(1, ngrp):
        spread(d).wait_recv()
    total = sums[g]
    for d in range(1, ngrp):
        total = total + arrived[d].astype(F32)
    moment = dot_nt(total.astype(BF16), maps[0]).astype(BF16)
    mom[...] = moment

    def share(d):
        return pltpu.make_async_remote_copy(
            src_ref=mom, dst_ref=mall.at[n], send_sem=m_send.at[d], recv_sem=m_recv.at[d],
            device_id=(cell(d), g), device_id_type=MESH)

    for d in range(1, ncell):
        share(d).start()
    mall[n] = moment

    for h in range(chunks):
        swap(h).wait_recv()

        @pl.when(forwards)
        def _():
            forward(h).start()

    w_pair[...] = jnp.zeros_like(w_pair)
    w_stack[...] = jnp.zeros_like(w_stack)
    scale[...] = jnp.zeros_like(scale)
    acc[...] = jnp.zeros_like(acc)

    @pl.loop(0, pairs)
    def _(j):
        for i in range(2):
            r = rot_ref[2 * j + i]
            w_pair[j, i * lanes:i * lanes + width, i * lanes:i * lanes + width] = r
            w_stack[j, i * lanes:i * lanes + width, :width] = r

    slot_id = lax.broadcasted_iota(jnp.int32, (slots, width), 0)
    for s in range(sd):
        live = jnp.where(slot_id < cnt_ref[s], 1.0, 0.0)
        scale[s, :, :width] = axial_ref[s].astype(F32) * live

    nbox = ncell * nbc
    row_box = lax.broadcasted_iota(jnp.int32, (rows, nbox), 0) // pq + n * nbc
    pick = (row_box == lax.broadcasted_iota(jnp.int32, (rows, nbox), 1)).astype(F32).astype(BF16)
    mine = jnp.dot(pick, coup_ref[...], preferred_element_type=F32).astype(BF16)
    for c in range(ncell):
        col_box = lax.broadcasted_iota(jnp.int32, (nbox, rows), 1) // pq + c * nbc
        put = (col_box == lax.broadcasted_iota(jnp.int32, (nbox, rows), 0)).astype(F32).astype(BF16)
        wide = jnp.dot(mine, put, preferred_element_type=F32)
        same = (lax.broadcasted_iota(jnp.int32, (rows, rows), 0) % pq
                == lax.broadcasted_iota(jnp.int32, (rows, rows), 1) % pq)
        lhs_c[c] = jnp.where(same, wide, 0.0).astype(BF16)

    @pl.when(receives)
    def _():
        for h in range(chunks):
            forward(h).wait_recv()

    block = 4

    def near(j):
        for sb in range(0, sd, block):
            lhs = jnp.concatenate([
                jnp.concatenate([cand[nbr_ref[s, 2 * j]], cand[nbr_ref[s, 2 * j + 1]]], axis=1)
                for s in range(sb, sb + block)], axis=0)
            turned = dot_nt(lhs, w_pair[j])
            scaled = jnp.concatenate([
                turned[(s - sb) * incid:(s - sb + 1) * incid]
                * jnp.concatenate([scale[s, pl.ds(2 * j, 1), :], scale[s, pl.ds(2 * j + 1, 1), :]], axis=1)
                for s in range(sb, sb + block)], axis=0).astype(BF16)
            acc[sb * incid:(sb + block) * incid, :] += jnp.dot(scaled, w_stack[j], preferred_element_type=F32)

    @pl.loop(0, pairs // 2)
    def _(j):
        near(j)

    for d in range(1, ncell):
        share(d).wait_recv()
    local = jnp.zeros((rows, lanes), F32)
    for c in range(ncell):
        local = local + jnp.dot(lhs_c[c], mall[c], preferred_element_type=F32)
    local = local.astype(BF16)
    loc[...] = local

    def spread_local(d):
        return pltpu.make_async_remote_copy(
            src_ref=loc, dst_ref=ball.at[g], send_sem=l_send.at[d], recv_sem=l_recv.at[d],
            device_id=(n, member(d)), device_id_type=MESH)

    for d in range(1, ngrp):
        spread_local(d).start()
    ball[g] = local

    @pl.loop(pairs // 2, pairs)
    def _(j):
        near(j)

    for d in range(1, ngrp):
        spread_local(d).wait_recv()
    for q in range(ngrp):
        far = dot_nt(ball[q], maps[1])
        for b in range(nbc):
            farbuf[b, q * pq:(q + 1) * pq, :] = far[b * pq:(b + 1) * pq]

    lane = lax.broadcasted_iota(jnp.int32, (incid, lanes), 1)
    fill = jnp.zeros((sd, lanes - width), F32)
    real_t = tmat_ref[:, :half]
    imag_t = tmat_ref[:, half:]
    same_t = jnp.concatenate([real_t, real_t, fill], axis=1)
    swap_t = jnp.concatenate([-imag_t, imag_t, fill], axis=1)
    for s in range(sd):
        u = acc[s * incid:(s + 1) * incid, :] + farbuf[box_ref[s]]
        turned = jnp.where(lane < half, pltpu.roll(u, lanes - half, 1), pltpu.roll(u, half, 1))
        v = same_t[s:s + 1] * u + swap_t[s:s + 1] * turned
        o_ref[s] = (x_ref[s].astype(F32) - v).astype(BF16)

    for h in range(chunks):
        swap(h).wait_send()

    @pl.when(forwards)
    def _():
        for h in range(chunks):
            forward(h).wait_send()

    for d in range(1, ngrp):
        spread(d).wait_send()
        spread_local(d).wait_send()
    for d in range(1, ncell):
        share(d).wait_send()


def shards(ncell, ngrp, coeffs, neighbours, counts, boxes, axial, rotations, out_map, coupling, in_map, tmat):
    sd, slots = neighbours.shape
    width = rotations.shape[1]
    incid = coeffs.shape[1] // width
    lanes = -(-width // 128) * 128
    nbc = NBG * ngrp
    pq = incid // ngrp
    rows = nbc * pq
    chunks = 4
    pairs = slots // 2
    x = jnp.pad(coeffs.reshape(sd, width, incid).transpose(0, 2, 1), ((0, 0), (0, 0), (0, lanes - width)))
    smem = pl.BlockSpec(memory_space=pltpu.SMEM)
    vmem = pl.BlockSpec(memory_space=pltpu.VMEM)
    dma = pltpu.SemaphoreType.DMA
    out = pl.pallas_call(
        functools.partial(kernel, (ncell, ngrp, chunks, sd, slots, width, incid, lanes, nbc, pq)),
        out_shape=jax.ShapeDtypeStruct((sd, incid, lanes), BF16),
        in_specs=[smem] * 3 + [vmem] * 7,
        out_specs=vmem,
        scratch_shapes=[
            pltpu.VMEM((3 * sd, incid, lanes), BF16),
            pltpu.VMEM((pairs, 2 * lanes, 2 * lanes), BF16),
            pltpu.VMEM((pairs, 2 * lanes, lanes), BF16),
            pltpu.VMEM((sd, slots, lanes), F32),
            pltpu.VMEM((sd * incid, lanes), F32),
            pltpu.VMEM((ngrp, rows, lanes), F32),
            pltpu.VMEM((ngrp, rows, lanes), BF16),
            pltpu.VMEM((ngrp, rows, lanes), BF16),
            pltpu.VMEM((rows, lanes), BF16),
            pltpu.VMEM((ncell, rows, lanes), BF16),
            pltpu.VMEM((ncell, rows, rows), BF16),
            pltpu.VMEM((rows, lanes), BF16),
            pltpu.VMEM((ngrp, rows, lanes), BF16),
            pltpu.VMEM((nbc, incid, lanes), F32),
            pltpu.VMEM((2, lanes, lanes), BF16),
            dma((chunks,)), dma((chunks,)), dma((chunks,)), dma((chunks,)),
            dma((ngrp,)), dma((ngrp,)), dma((ncell,)), dma((ncell,)), dma((ngrp,)), dma((ngrp,)),
        ],
        compiler_params=pltpu.CompilerParams(collective_id=0, has_side_effects=True),
    )(neighbours, counts, boxes, x, axial, rotations, out_map, coupling, in_map, tmat)
    return out[:, :, :width].transpose(0, 2, 1).reshape(sd, width * incid)


def solution(mesh):
    in_specs = (
        P(("cells", "grp"), None),
        P(("cells", "grp"), None),
        P(("cells", "grp")),
        P(("cells", "grp")),
        P(("cells", "grp"), None, None),
        P(),
        P(),
        P(),
        P(),
        P(("cells", "grp"), None),
    )
    out_specs = P(("cells", "grp"), None)
    body = functools.partial(shards, mesh.shape["cells"], mesh.shape["grp"])
    return jax.shard_map(body, mesh=mesh, in_specs=in_specs, out_specs=out_specs, check_vma=False)
```

time: 148 us -> 39.7 us (0.27)
  the two profiles are of different devices: /device:TPU:0 before, /device:TPU:17 now
where the time goes in v1:
time: 39.7 us; the launch traced here: 39.5 us
  Pallas kernels  35 us (88%)
  local copies, waits for them, and re-layouts  4.53 us (11%)
    pallas_call x1, Pallas kernels, shards(): pl.pallas_call(functools.partial(kernel, (ncell, ngrp, chunks, sd, slots,...  35 us
    reshape x2, local copies, waits for them, and re-layouts, shards(): coeffs.reshape(sd, width, incid).transpose(0, 2, 1)  1.53 us
    transpose x2, local copies, waits for them, and re-layouts, shards(): return out[:, :, :width].transpose(0, 2, 1).reshape(sd, width * incid)  1.19 us
    reshape x1, local copies, waits for them, and re-layouts, shards(): return out[:, :, :width].transpose(0, 2, 1).reshape(sd, width * incid)  1.05 us

profile of v1, /device:TPU:17, one launch (start us, length us, event | category | flops | bytes accessed | tf_op | source)
XLA Modules:
  0.0 39.5 jit_solution(12165796810242625702)
XLA Ops:
  0.0 1.3 %reshape.6 = bf16[16,96,64]{2,1,0:T(8,128)(2,1)S(1)} reshape(bf16[16,6144]{1,0:T(8,128)(2,1)} %param.10) | data formatting | bytes 393216 | tf_op jit(solution)/shard_map/reshape | solution.py:236
  1.3 0.2 copy.11
  1.5 0.8 %pad.4.x_ref = bf16[16,64,128]{2,1,0:T(8,128)(2,1)} pad(bf16[16,64,96]{2,1,0:T(8,128)(2,1)S(1)} %bitcast.3, bf16[]{:T(256)} %constant.2.clone.1), padding=0_0x0_0x0_32 | pad | bytes 458754 | tf_op jit(solution)/shard_map/jit(_pad)/pad | solution.py:236
  2.3 35.0 %shard_map.100 = bf16[16,64,128]{2,1,0:T(8,128)(2,1)} custom-call(s32[16,32]{1,0:T(8,128)} %nbr_ref.1, s32[16]{0:T(128)} %cnt_ref.1, s32[16]{0:T(128)} %box_ref.1, bf16[16,64,128]{2,1,0:T(8,128)(2,1)} %pad.4.x_ref, bf16[16,32,96]{2,1,0:T(8,128)(2,1)} %axial_ref.1, bf16[32,96,96]{2,1,0:T(8,128)(2,1)} %rot_ref.1, bf16[96,96]{1,0:T(8,128)(2,1)} %out_map_ref.1, ...), custom_call_target="tpu_custom_call" | custom-call | tf_op jit(solution)/shard_map/pallas_call | solution.py:240
  37.3 1.0 %slice_bitcast_fusion = bf16[16,96,64]{1,2,0:T(8,128)(2,1)S(1)} fusion(bf16[16,64,128]{2,1,0:T(8,128)(2,1)} %shard_map.100), kind=kLoop, calls=%fused_computation | loop fusion | bytes 393216 | tf_op jit(solution)/shard_map/transpose | solution.py:266
  38.3 0.2 copy.12
  38.5 1.0 %reshape.7 = bf16[16,6144]{1,0:T(8,128)(2,1)} reshape(bf16[16,96,64]{2,1,0:T(8,128)(2,1)S(1)} %copy.12) | data formatting | bytes 393216 | tf_op jit(solution)/shard_map/reshape | solution.py:266

commit v2 on v1

--- a/solution.py
+++ b/solution.py
@@ -18,7 +18,7 @@
 
 
 def kernel(dims, nbr_ref, cnt_ref, box_ref, x_ref, axial_ref, rot_ref, out_map_ref, coup_ref, in_map_ref, tmat_ref,
-           o_ref, cand, w_pair, w_stack, scale, acc, sums, part, arrived, mom, mall, lhs_c, loc, ball, farbuf, maps,
+           o_ref, cand, raw, flat_sums, box_rows, rows_own, rows_near, rows_other, w_pair, w_stack, scale, acc, sums, part, arrived, mom, mall, lhs_c, loc, ball, farbuf, maps,
            h_send, h_recv, f_send, f_recv, a_send, a_recv, m_send, m_recv, l_send, l_recv):
     ncell, ngrp, chunks, sd, slots, width, incid, lanes, nbc, pq = dims
     half = width // 2
@@ -34,7 +34,8 @@
     receives = jnp.logical_and(source >= 0, source < ncell)
     near_slot = 2 * (1 - par)
     other_slot = 2 * par
-    step = sd // chunks
+    group = sd * 2 // chunks
+    flat = width * incid
 
     def cell(d):
         return lax.rem(n + d, ncell)
@@ -49,26 +50,46 @@
         pl.semaphore_signal(barrier, inc=1, device_id=(n, member(d)), device_id_type=MESH)
     pl.semaphore_wait(barrier, ncell + ngrp - 2)
 
+    def piece(h):
+        return pl.ds(h // 2 * group, group), pl.ds(h % 2 * (flat // 2), flat // 2)
+
     def swap(h):
         return pltpu.make_async_remote_copy(
-            src_ref=x_ref.at[pl.ds(h * step, step)], dst_ref=cand.at[pl.ds(other_slot * sd + h * step, step)],
+            src_ref=x_ref.at[piece(h)], dst_ref=raw.at[(par,) + piece(h)],
             send_sem=h_send.at[h], recv_sem=h_recv.at[h], device_id=(partner, g), device_id_type=MESH)
 
     def forward(h):
         return pltpu.make_async_remote_copy(
-            src_ref=cand.at[pl.ds(near_slot * sd + h * step, step)],
-            dst_ref=cand.at[pl.ds(other_slot * sd + h * step, step)],
+            src_ref=raw.at[(1 - par,) + piece(h)], dst_ref=raw.at[(par,) + piece(h)],
             send_sem=f_send.at[h], recv_sem=f_recv.at[h], device_id=(onward, g), device_id_type=MESH)
 
     for h in range(chunks):
         swap(h).start()
 
-    xs = [x_ref[s].astype(F32) for s in range(sd)]
+    per = lanes // incid
+    tiles = flat // lanes
+    below = jnp.zeros((lanes - width, lanes), F32)
+
+    def lay_rows(load, dst, r, span):
+        for t in span:
+            v = load(t)
+            for i in range(per):
+                dst[pl.ds(r * group * width + t * per + i, group, stride=width), :] = (
+                    v if i == 0 else pltpu.roll(v, lanes - i * incid, 1))
+
+    def turned_block(src, s):
+        return jnp.concatenate([src[s * width:(s + 1) * width, :], below], axis=0).T[:incid]
+
+    box_of = jnp.zeros((nbc, sd), jnp.int32)
+    column = lax.broadcasted_iota(jnp.int32, (nbc, sd), 1)
+    for s in range(sd):
+        box_of = jnp.where(column == s, box_ref[s], box_of)
+    onehot = (box_of == lax.broadcasted_iota(jnp.int32, (nbc, sd), 0)).astype(F32).astype(BF16)
+    flat_sums[...] = jnp.dot(onehot, x_ref[...], preferred_element_type=F32)
+    for r in range(nbc // group):
+        lay_rows(lambda t: flat_sums[r * group:(r + 1) * group, t * lanes:(t + 1) * lanes], box_rows, r, range(tiles))
     for b in range(nbc):
-        total = None
-        for s in range(sd):
-            term = xs[s] * jnp.where(box_ref[s] == b, 1.0, 0.0)
-            total = term if total is None else total + term
+        total = turned_block(box_rows, b)
         for q in range(ngrp):
             sums[q, b * pq:(b + 1) * pq, :] = total[q * pq:(q + 1) * pq]
     for q in range(ngrp):
@@ -82,7 +103,11 @@
     for d in range(1, ngrp):
         spread(d).start()
 
-    cand[sd:2 * sd] = x_ref[...]
+    for r in range(sd // group):
+        lay_rows(lambda t: x_ref[r * group:(r + 1) * group, t * lanes:(t + 1) * lanes].astype(F32),
+                 rows_own, r, range(tiles))
+    for s in range(sd):
+        cand[sd + s] = turned_block(rows_own, s).astype(BF16)
 
     @pl.when(jnp.logical_not(receives))
     def _():
@@ -97,7 +122,9 @@
     total = sums[g]
     for d in range(1, ngrp):
         total = total + arrived[d].astype(F32)
-    moment = dot_nt(total.astype(BF16), maps[0]).astype(BF16)
+    high = total.astype(BF16)
+    low = (total - high.astype(F32)).astype(BF16)
+    moment = (dot_nt(high, maps[0]) + dot_nt(low, maps[0])).astype(BF16)
     mom[...] = moment
 
     def share(d):
@@ -145,10 +172,22 @@
                 == lax.broadcasted_iota(jnp.int32, (rows, rows), 1) % pq)
         lhs_c[c] = jnp.where(same, wide, 0.0).astype(BF16)
 
+    def take(copy, slot, rows_of, place):
+        for h in range(chunks):
+            if copy is not None:
+                copy(h).wait_recv()
+            r = h // 2
+            lay_rows(lambda t: raw[slot, r * group:(r + 1) * group, t * lanes:(t + 1) * lanes].astype(F32),
+                     rows_of, r, range(h % 2 * (tiles // 2), (h % 2 + 1) * (tiles // 2)))
+            if h % 2 == 1:
+                for s in range(r * group, (r + 1) * group):
+                    cand[place * sd + s] = turned_block(rows_of, s).astype(BF16)
+
+    take(None, 1 - par, rows_near, near_slot)
+
     @pl.when(receives)
     def _():
-        for h in range(chunks):
-            forward(h).wait_recv()
+        take(forward, par, rows_other, other_slot)
 
     block = 4
 
@@ -164,9 +203,10 @@
                 for s in range(sb, sb + block)], axis=0).astype(BF16)
             acc[sb * incid:(sb + block) * incid, :] += jnp.dot(scaled, w_stack[j], preferred_element_type=F32)
 
-    @pl.loop(0, pairs // 2)
+    @pl.loop(0, pairs // 4)
     def _(j):
-        near(j)
+        near(2 * j)
+        near(2 * j + 1)
 
     for d in range(1, ncell):
         share(d).wait_recv()
@@ -185,9 +225,10 @@
         spread_local(d).start()
     ball[g] = local
 
-    @pl.loop(pairs // 2, pairs)
+    @pl.loop(pairs // 4, pairs // 2)
     def _(j):
-        near(j)
+        near(2 * j)
+        near(2 * j + 1)
 
     for d in range(1, ngrp):
         spread_local(d).wait_recv()
@@ -206,7 +247,16 @@
         u = acc[s * incid:(s + 1) * incid, :] + farbuf[box_ref[s]]
         turned = jnp.where(lane < half, pltpu.roll(u, lanes - half, 1), pltpu.roll(u, half, 1))
         v = same_t[s:s + 1] * u + swap_t[s:s + 1] * turned
-        o_ref[s] = (x_ref[s].astype(F32) - v).astype(BF16)
+        own = (cand[sd + s].astype(F32) - v).astype(BF16).astype(F32)
+        own = jnp.concatenate([own, jnp.zeros((lanes - incid, lanes), F32)], axis=0)
+        rows_own[s * width:(s + 1) * width, :] = own.T[:width]
+    for r in range(sd // group):
+        for t in range(tiles):
+            v = None
+            for i in range(per):
+                got = rows_own[pl.ds(r * group * width + t * per + i, group, stride=width), :]
+                v = got if v is None else v + pltpu.roll(got, i * incid, 1)
+            o_ref[r * group:(r + 1) * group, t * lanes:(t + 1) * lanes] = v.astype(BF16)
 
     for h in range(chunks):
         swap(h).wait_send()
@@ -231,19 +281,25 @@
     nbc = NBG * ngrp
     pq = incid // ngrp
     rows = nbc * pq
-    chunks = 4
+    chunks = sd // 8 * 2
+    flat = width * incid
     pairs = slots // 2
-    x = jnp.pad(coeffs.reshape(sd, width, incid).transpose(0, 2, 1), ((0, 0), (0, 0), (0, lanes - width)))
     smem = pl.BlockSpec(memory_space=pltpu.SMEM)
     vmem = pl.BlockSpec(memory_space=pltpu.VMEM)
     dma = pltpu.SemaphoreType.DMA
-    out = pl.pallas_call(
+    return pl.pallas_call(
         functools.partial(kernel, (ncell, ngrp, chunks, sd, slots, width, incid, lanes, nbc, pq)),
-        out_shape=jax.ShapeDtypeStruct((sd, incid, lanes), BF16),
+        out_shape=jax.ShapeDtypeStruct((sd, flat), BF16),
         in_specs=[smem] * 3 + [vmem] * 7,
         out_specs=vmem,
         scratch_shapes=[
             pltpu.VMEM((3 * sd, incid, lanes), BF16),
+            pltpu.VMEM((2, sd, flat), BF16),
+            pltpu.VMEM((nbc, flat), F32),
+            pltpu.VMEM((nbc * width, lanes), F32),
+            pltpu.VMEM((sd * width, lanes), F32),
+            pltpu.VMEM((sd * width, lanes), F32),
+            pltpu.VMEM((sd * width, lanes), F32),
             pltpu.VMEM((pairs, 2 * lanes, 2 * lanes), BF16),
             pltpu.VMEM((pairs, 2 * lanes, lanes), BF16),
             pltpu.VMEM((sd, slots, lanes), F32),
@@ -262,8 +318,7 @@
             dma((ngrp,)), dma((ngrp,)), dma((ncell,)), dma((ncell,)), dma((ngrp,)), dma((ngrp,)),
         ],
         compiler_params=pltpu.CompilerParams(collective_id=0, has_side_effects=True),
-    )(neighbours, counts, boxes, x, axial, rotations, out_map, coupling, in_map, tmat)
-    return out[:, :, :width].transpose(0, 2, 1).reshape(sd, width * incid)
+    )(neighbours, counts, boxes, coeffs, axial, rotations, out_map, coupling, in_map, tmat)
 
 
 def solution(mesh):

time: 39.7 us -> 33 us (0.83)
  Pallas kernels: 35 us -> 31.2 us
  local copies, waits for them, and re-layouts: 4.53 us -> 1.62 us
    pallas_call x1, Pallas kernels: 35 us -> 31.2 us  [shards(): pl.pallas_call(functools.partial(kernel, (ncell, ngrp, chunks, sd, slots,...]
    reshape x3 -> x0, local copies, waits for them, and re-layouts: 2.58 us -> none  [the longest x2 1.53 us: shards(): coeffs.reshape(sd, width, incid).transpose(0, 2, 1)]
    unnamed x0 -> x1, local copies, waits for them, and re-layouts: none -> 1.62 us
    transpose x2 -> x0, local copies, waits for them, and re-layouts: 1.19 us -> none  [shards(): return out[:, :, :width].transpose(0, 2, 1).reshape(sd, width * incid)]
    pad x1 -> x0, local copies, waits for them, and re-layouts: 0.76 us -> none  [shards(): jnp.pad(coeffs.reshape(sd, width, incid).transpose(0, 2, 1), ((0, 0), (0,...]
where the time goes in v2:
time: 33 us; the launch traced here: 32.9 us
  Pallas kernels  31.2 us (95%)
  local copies, waits for them, and re-layouts  1.62 us (5%)
    pallas_call x1, Pallas kernels, shards(): pl.pallas_call(functools.partial(kernel, (ncell, ngrp, chunks, sd, slots,...  31.2 us
    unnamed x1, local copies, waits for them, and re-layouts  1.62 us

profile of v2, /device:TPU:17, one launch (start us, length us, event | category | flops | bytes accessed | tf_op | source)
XLA Modules:
  0.0 32.9 jit_solution(13680876661983858397)
XLA Ops:
  0.0 31.2 %shard_map.100 = bf16[16,6144]{1,0:T(8,128)(2,1)} custom-call(s32[16,32]{1,0:T(8,128)} %nbr_ref.1, s32[16]{0:T(128)} %cnt_ref.1, s32[16]{0:T(128)} %box_ref.1, bf16[16,6144]{1,0:T(8,128)(2,1)} %x_ref.1, bf16[16,32,96]{2,1,0:T(8,128)(2,1)} %axial_ref.1, bf16[32,96,96]{2,1,0:T(8,128)(2,1)} %rot_ref.1, bf16[96,96]{1,0:T(8,128)(2,1)} %out_map_ref.1, ...), custom_call_target="tpu_custom_call" | custom-call | tf_op jit(solution)/shard_map/pallas_call | solution.py:290
  31.2 1.6 %copy.12 = bf16[16,6144]{1,0:T(8,128)(2,1)} copy(bf16[16,6144]{1,0:T(8,128)(2,1)} %shard_map.100) | data formatting | bytes 393216

commit v3 on v2

--- a/solution.py
+++ b/solution.py
@@ -19,7 +19,7 @@
 
 def kernel(dims, nbr_ref, cnt_ref, box_ref, x_ref, axial_ref, rot_ref, out_map_ref, coup_ref, in_map_ref, tmat_ref,
            o_ref, cand, raw, flat_sums, box_rows, rows_own, rows_near, rows_other, w_pair, w_stack, scale, acc, sums, part, arrived, mom, mall, lhs_c, loc, ball, farbuf, maps,
-           h_send, h_recv, f_send, f_recv, a_send, a_recv, m_send, m_recv, l_send, l_recv):
+           h_send, h_recv, f_send, f_recv, a_send, a_recv, m_send, m_recv, l_send, l_recv, g_send, g_recv, giving, given):
     ncell, ngrp, chunks, sd, slots, width, incid, lanes, nbc, pq = dims
     half = width // 2
     rows = nbc * pq
@@ -37,18 +37,22 @@
     group = sd * 2 // chunks
     flat = width * incid
 
+    nhalf = ncell // 2
+    mine_at = n // 2
+
     def cell(d):
-        return lax.rem(n + d, ncell)
+        return par + 2 * lax.rem(mine_at + d, nhalf)
 
     def member(d):
         return lax.rem(g + d, ngrp)
 
     barrier = pltpu.get_barrier_semaphore()
-    for d in range(1, ncell):
+    for d in range(1, nhalf):
         pl.semaphore_signal(barrier, inc=1, device_id=(cell(d), g), device_id_type=MESH)
+    pl.semaphore_signal(barrier, inc=1, device_id=(partner, g), device_id_type=MESH)
     for d in range(1, ngrp):
         pl.semaphore_signal(barrier, inc=1, device_id=(n, member(d)), device_id_type=MESH)
-    pl.semaphore_wait(barrier, ncell + ngrp - 2)
+    pl.semaphore_wait(barrier, nhalf + ngrp - 1)
 
     def piece(h):
         return pl.ds(h // 2 * group, group), pl.ds(h % 2 * (flat // 2), flat // 2)
@@ -117,6 +121,13 @@
         maps[m] = jnp.zeros((lanes, lanes), BF16)
         maps[m, :width, :width] = ref[...]
 
+    for h in range(chunks // 2):
+        swap(h).wait_recv()
+
+        @pl.when(forwards)
+        def _():
+            forward(h).start()
+
     for d in range(1, ngrp):
         spread(d).wait_recv()
     total = sums[g]
@@ -129,14 +140,14 @@
 
     def share(d):
         return pltpu.make_async_remote_copy(
-            src_ref=mom, dst_ref=mall.at[n], send_sem=m_send.at[d], recv_sem=m_recv.at[d],
+            src_ref=mom, dst_ref=mall.at[mine_at], send_sem=m_send.at[d], recv_sem=m_recv.at[d],
             device_id=(cell(d), g), device_id_type=MESH)
 
-    for d in range(1, ncell):
+    for d in range(1, nhalf):
         share(d).start()
-    mall[n] = moment
-
-    for h in range(chunks):
+    mall[mine_at] = moment
+
+    for h in range(chunks // 2, chunks):
         swap(h).wait_recv()
 
         @pl.when(forwards)
@@ -161,16 +172,17 @@
         scale[s, :, :width] = axial_ref[s].astype(F32) * live
 
     nbox = ncell * nbc
-    row_box = lax.broadcasted_iota(jnp.int32, (rows, nbox), 0) // pq + n * nbc
-    pick = (row_box == lax.broadcasted_iota(jnp.int32, (rows, nbox), 1)).astype(F32).astype(BF16)
-    mine = jnp.dot(pick, coup_ref[...], preferred_element_type=F32).astype(BF16)
-    for c in range(ncell):
-        col_box = lax.broadcasted_iota(jnp.int32, (nbox, rows), 1) // pq + c * nbc
-        put = (col_box == lax.broadcasted_iota(jnp.int32, (nbox, rows), 0)).astype(F32).astype(BF16)
-        wide = jnp.dot(mine, put, preferred_element_type=F32)
-        same = (lax.broadcasted_iota(jnp.int32, (rows, rows), 0) % pq
-                == lax.broadcasted_iota(jnp.int32, (rows, rows), 1) % pq)
-        lhs_c[c] = jnp.where(same, wide, 0.0).astype(BF16)
+    same = (lax.broadcasted_iota(jnp.int32, (rows, rows), 0) % pq
+            == lax.broadcasted_iota(jnp.int32, (rows, rows), 1) % pq)
+    for k, target in enumerate((n, partner)):
+        row_box = lax.broadcasted_iota(jnp.int32, (rows, nbox), 0) // pq + target * nbc
+        pick = (row_box == lax.broadcasted_iota(jnp.int32, (rows, nbox), 1)).astype(F32).astype(BF16)
+        chosen = jnp.dot(pick, coup_ref[...], preferred_element_type=F32).astype(BF16)
+        for m in range(nhalf):
+            col_box = lax.broadcasted_iota(jnp.int32, (nbox, rows), 1) // pq + (par + 2 * m) * nbc
+            put = (col_box == lax.broadcasted_iota(jnp.int32, (nbox, rows), 0)).astype(F32).astype(BF16)
+            wide = jnp.dot(chosen, put, preferred_element_type=F32)
+            lhs_c[k, m] = jnp.where(same, wide, 0.0).astype(BF16)
 
     def take(copy, slot, rows_of, place):
         for h in range(chunks):
@@ -184,6 +196,19 @@
                     cand[place * sd + s] = turned_block(rows_of, s).astype(BF16)
 
     take(None, 1 - par, rows_near, near_slot)
+
+    def give():
+        return pltpu.make_async_remote_copy(
+            src_ref=giving, dst_ref=given, send_sem=g_send, recv_sem=g_recv,
+            device_id=(partner, g), device_id_type=MESH)
+
+    for d in range(1, nhalf):
+        share(d).wait_recv()
+    partial = jnp.dot(lhs_c[1, 0], mall[0], preferred_element_type=F32)
+    for m in range(1, nhalf):
+        partial = partial + jnp.dot(lhs_c[1, m], mall[m], preferred_element_type=F32)
+    giving[...] = partial
+    give().start()
 
     @pl.when(receives)
     def _():
@@ -203,16 +228,15 @@
                 for s in range(sb, sb + block)], axis=0).astype(BF16)
             acc[sb * incid:(sb + block) * incid, :] += jnp.dot(scaled, w_stack[j], preferred_element_type=F32)
 
-    @pl.loop(0, pairs // 4)
+    @pl.loop(0, pairs // 16)
     def _(j):
-        near(2 * j)
-        near(2 * j + 1)
-
-    for d in range(1, ncell):
-        share(d).wait_recv()
-    local = jnp.zeros((rows, lanes), F32)
-    for c in range(ncell):
-        local = local + jnp.dot(lhs_c[c], mall[c], preferred_element_type=F32)
+        for i in range(8):
+            near(8 * j + i)
+
+    give().wait_recv()
+    local = given[...]
+    for m in range(nhalf):
+        local = local + jnp.dot(lhs_c[0, m], mall[m], preferred_element_type=F32)
     local = local.astype(BF16)
     loc[...] = local
 
@@ -225,10 +249,10 @@
         spread_local(d).start()
     ball[g] = local
 
-    @pl.loop(pairs // 4, pairs // 2)
+    @pl.loop(pairs // 16, pairs // 8)
     def _(j):
-        near(2 * j)
-        near(2 * j + 1)
+        for i in range(8):
+            near(8 * j + i)
 
     for d in range(1, ngrp):
         spread_local(d).wait_recv()
@@ -269,8 +293,9 @@
     for d in range(1, ngrp):
         spread(d).wait_send()
         spread_local(d).wait_send()
-    for d in range(1, ncell):
+    for d in range(1, nhalf):
         share(d).wait_send()
+    give().wait_send()
 
 
 def shards(ncell, ngrp, coeffs, neighbours, counts, boxes, axial, rotations, out_map, coupling, in_map, tmat):
@@ -308,14 +333,16 @@
             pltpu.VMEM((ngrp, rows, lanes), BF16),
             pltpu.VMEM((ngrp, rows, lanes), BF16),
             pltpu.VMEM((rows, lanes), BF16),
-            pltpu.VMEM((ncell, rows, lanes), BF16),
-            pltpu.VMEM((ncell, rows, rows), BF16),
+            pltpu.VMEM((ncell // 2, rows, lanes), BF16),
+            pltpu.VMEM((2, ncell // 2, rows, rows), BF16),
             pltpu.VMEM((rows, lanes), BF16),
             pltpu.VMEM((ngrp, rows, lanes), BF16),
             pltpu.VMEM((nbc, incid, lanes), F32),
             pltpu.VMEM((2, lanes, lanes), BF16),
             dma((chunks,)), dma((chunks,)), dma((chunks,)), dma((chunks,)),
-            dma((ngrp,)), dma((ngrp,)), dma((ncell,)), dma((ncell,)), dma((ngrp,)), dma((ngrp,)),
+            dma((ngrp,)), dma((ngrp,)), dma((ncell,)), dma((ncell,)), dma((ngrp,)), dma((ngrp,)), dma, dma,
+            pltpu.VMEM((rows, lanes), F32),
+            pltpu.VMEM((rows, lanes), F32),
         ],
         compiler_params=pltpu.CompilerParams(collective_id=0, has_side_effects=True),
     )(neighbours, counts, boxes, coeffs, axial, rotations, out_map, coupling, in_map, tmat)

time: 33 us -> 27.4 us (0.83)
  the two profiles are of different devices: /device:TPU:17 before, /device:TPU:0 now
where the time goes in v3:
time: 27.4 us; the launch traced here: 27.2 us
  Pallas kernels  25.6 us (93%)
  local copies, waits for them, and re-layouts  1.62 us (6%)
    pallas_call x1, Pallas kernels, shards(): pl.pallas_call(functools.partial(kernel, (ncell, ngrp, chunks, sd, slots,...  25.6 us
    unnamed x1, local copies, waits for them, and re-layouts  1.62 us

profile of v3, /device:TPU:0, one launch (start us, length us, event | category | flops | bytes accessed | tf_op | source)
XLA Modules:
  0.0 27.2 jit_solution(10260289853021606299)
XLA Ops:
  0.0 25.6 %shard_map.100 = bf16[16,6144]{1,0:T(8,128)(2,1)} custom-call(s32[16,32]{1,0:T(8,128)} %nbr_ref.1, s32[16]{0:T(128)} %cnt_ref.1, s32[16]{0:T(128)} %box_ref.1, bf16[16,6144]{1,0:T(8,128)(2,1)} %x_ref.1, bf16[16,32,96]{2,1,0:T(8,128)(2,1)} %axial_ref.1, bf16[32,96,96]{2,1,0:T(8,128)(2,1)} %rot_ref.1, bf16[96,96]{1,0:T(8,128)(2,1)} %out_map_ref.1, ...), custom_call_target="tpu_custom_call" | custom-call | tf_op jit(solution)/shard_map/pallas_call | solution.py:315
  25.6 1.6 %copy.12 = bf16[16,6144]{1,0:T(8,128)(2,1)} copy(bf16[16,6144]{1,0:T(8,128)(2,1)} %shard_map.100) | data formatting | bytes 393216
